TPU v7x, 512 devices: a whole 4x4x16 slice. The times are simulated.
512 devices in a mesh: half: 2 (over z_hi), row: 8 (over y, core), col: 32 (over x, z_lo).
Axes of the slice: x: 4, y: 4, z: 16 (z_hi: 2, z_lo: 8; z = z_hi * 8 + z_lo), core: 2. Of those that a mesh axis runs over, the one named last changes fastest.
Arguments:
- child_updates: float32 [2, 8192, 8192], P('half', 'row', 'col'), may hold values from -6 to 6
- child_maps: int32 [2, 64], replicated, may hold values from 0 to 95, as said below
- panel_pattern: int32 [96, 6], replicated, may hold values 0 or 1
- pivot_inverse: float32 [768, 768], replicated, may hold values from -1 to 1, as said below
Outputs:
- front_out: float32 [8, 2, 768, 12288], P('row', 'half', None, 'col')
Inputs may be any that keep to these rules, and one draw needn't show every extreme that they name: child_maps[c, 2 m] and child_maps[c, 2 m + 1] are two different values of 3 m, 3 m + 1, 3 m + 2, the smaller first. `pivot_inverse`: lower triangular with a positive diagonal.
All inputs are finite; a program needn't handle non-finite values.
Results may differ from a plain program's by a relative error of at most 0.000086.
Values sent between devices are 32-bit elements; how exact they have to be, the bound alone decides.
A program may use at most 64 MiB of HBM per device.

v0:
```python
import jax
import jax.numpy as jnp
from jax import lax
from jax.sharding import PartitionSpec as P

BLK = 128
P_SIZE = 768
NF = 12288


def broadcast(block, axis, source):
    block = jnp.where(lax.axis_index(axis) == source, block, jnp.zeros_like(block))
    return lax.psum(block, axis)


def expand_tile(
    child_tile, block_map, child_row0, child_col0, parent_row0, parent_col0, out_rows, out_cols
):
    row_blocks = child_tile.shape[0] // BLK
    col_blocks = child_tile.shape[1] // BLK
    row_target = lax.dynamic_slice_in_dim(block_map, child_row0, row_blocks) - parent_row0
    col_target = lax.dynamic_slice_in_dim(block_map, child_col0, col_blocks) - parent_col0
    row_onehot = (row_target[:, None] == jnp.arange(out_rows, dtype=jnp.int32)[None, :]).astype(
        jnp.float32
    )
    col_onehot = (col_target[:, None] == jnp.arange(out_cols, dtype=jnp.int32)[None, :]).astype(
        jnp.float32
    )
    blocks = child_tile.reshape(row_blocks, BLK, col_blocks, BLK)
    placed = jnp.einsum("axby,bq->axqy", blocks, col_onehot, precision=lax.Precision.HIGHEST)
    placed = jnp.einsum("ap,axqy->pxqy", row_onehot, placed, precision=lax.Precision.HIGHEST)
    return placed.reshape(out_rows * BLK, out_cols * BLK)


def local(child_updates, child_maps, panel_pattern, pivot_inverse):
    child_tile = child_updates[0]
    row_count = lax.axis_size("row")
    col_count = lax.axis_size("col")
    half_index = lax.axis_index("half")
    row_index = lax.axis_index("row")
    col_index = lax.axis_index("col")
    slab_rows = NF // (2 * row_count)
    slab_cols = NF // col_count
    child_rows = child_tile.shape[0] // BLK
    child_cols = child_tile.shape[1] // BLK
    own_map = lax.dynamic_index_in_dim(child_maps, half_index, 0, keepdims=False)
    slab_index = 2 * row_index + half_index
    col_first = col_index * (slab_cols // BLK)
    own_terms = expand_tile(
        child_tile,
        own_map,
        row_index * child_rows,
        col_index * child_cols,
        row_index * (2 * slab_rows // BLK),
        col_first,
        2 * slab_rows // BLK,
        slab_cols // BLK,
    )
    assembled = lax.psum_scatter(own_terms, "half", scatter_dimension=0, tiled=True)
    owner_count = -(-P_SIZE // slab_cols)
    pieces = [broadcast(assembled, "col", owner) for owner in range(owner_count)]
    panel_cols = jnp.concatenate(pieces, axis=1)
    pattern_rows = lax.dynamic_slice_in_dim(
        panel_pattern, slab_index * (slab_rows // BLK), slab_rows // BLK, 0
    )
    pattern_mask = jnp.repeat(jnp.repeat(pattern_rows, BLK, axis=0), BLK, axis=1).astype(
        jnp.float32
    )
    factor = jnp.dot(panel_cols, pivot_inverse.T, precision=lax.Precision.HIGHEST) * pattern_mask
    col_start = col_index * slab_cols
    source_slab = col_start // slab_rows
    root_device = row_count * (source_slab % 2) + source_slab // 2
    sent_rows = lax.dynamic_slice_in_dim(factor, col_start % slab_rows, slab_cols, 0)
    column_factor = broadcast(sent_rows, ("half", "row"), root_device)
    schur_term = jnp.dot(factor, column_factor.T, precision=lax.Precision.HIGHEST)
    padded_factor = jnp.pad(factor, ((0, 0), (0, slab_cols)))
    factor_cols = lax.dynamic_slice_in_dim(
        padded_factor, jnp.minimum(col_start, P_SIZE), slab_cols, 1
    )
    global_rows = slab_index * slab_rows + jnp.arange(slab_rows, dtype=jnp.int32)[:, None]
    global_cols = col_start + jnp.arange(slab_cols, dtype=jnp.int32)[None, :]
    result = jnp.where(
        global_cols < P_SIZE,
        factor_cols,
        jnp.where(global_rows < P_SIZE, assembled, assembled - schur_term),
    )
    return result.reshape(1, 1, slab_rows, slab_cols)


def solution(mesh):
    placed = (P("half", "row", "col"), P(), P(), P())
    return jax.shard_map(
        local, mesh=mesh, in_specs=placed, out_specs=P("row", "half", None, "col"), check_vma=False
    )
```

profile of v0, /device:TPU:1, one launch (start us, length us, event | category | flops | bytes accessed | tf_op | source)
XLA Modules:
  0.0 906.2 jit_solution(6084546498089460596)
XLA Ops:
  6.5 0.0 copy-start
  6.5 0.0 reduce-scatter.2.cloned.1.call-start
  6.5 1.9 reshape_squeeze.3
  8.5 0.0 copy-done.4
  8.5 0.1 subtract_bitcast_fusion
  8.6 3.7 fusion.14
  12.3 3.2 copy.14
  15.5 0.1 subtract_bitcast_fusion.1
  15.6 3.0 fusion.7
  18.6 2.5 copy.19
  21.1 3.1 copy.7
  24.2 0.0 reduce-scatter.2.cloned.1.call-update
  24.2 0.0 all-reduce.7.cloned.1.call-start
  24.2 123.8 %reduce-scatter.2.cloned.1.call-done = f32[768,384]{1,0:T(8,128)} async-done(((f32[1536,384]{1,0:T(8,128)}), f32[768,384]{1,0:T(8,128)}) %reduce-scatter.2.cloned.1.call-update) | async-done | bytes 1179664 | tf_op jit(solution)/shard_map/reduce_scatter | solution.py:59
  148.1 2.9 broadcast_select_fusion.1
  151.0 0.0 all-reduce.7.cloned.1.call-update
  151.0 0.2 all-reduce.5.cloned.1.call-start
  151.3 0.4 copy-done.3
  151.7 0.1 dynamic-slice_convert_fusion
  151.8 0.1 broadcast_bitcast_fusion
  151.8 1.6 broadcast_in_dim.33
  153.4 3.1 copy.8
  156.5 444.8 %all-reduce.7.cloned.1.call-done = (f32[768,384]{1,0:T(8,128)}, f32[768,384]{1,0:T(8,128)}) async-done(((f32[768,384]{1,0:T(8,128)}, f32[768,384]{1,0:T(8,128)}), (f32[768,384]{1,0:T(8,128)}, f32[768,384]{1,0:T(8,128)})) %all-reduce.7.cloned.1.call-update) | async-done | bytes 2359312 | tf_op jit(solution)/shard_map/psum | solution.py:13
  601.3 0.0 copy-done
  601.3 7.9 fusion.4
  609.1 0.0 copy-start.1
  609.2 1.4 copy-done.1
  610.6 1.1 dynamic-slice_select_fusion
  611.7 0.0 all-reduce.5.cloned.1.call-update
  611.8 280.6 %all-reduce.5.cloned.1.call-done = f32[384,768]{1,0:T(8,128)} async-done(((f32[384,768]{1,0:T(8,128)}), f32[384,768]{1,0:T(8,128)}) %all-reduce.5.cloned.1.call-update) | async-done | bytes 1179664 | tf_op jit(solution)/shard_map/psum | solution.py:13
  892.3 0.0 copy-done.2
  892.3 7.3 fusion.10
  (6 shorter events, 0.0 us)
Async XLA Ops:
  6.5 594.7 %copy-start = (f32[768,768]{1,0:T(8,128)S(1)}, f32[768,768]{1,0:T(8,128)}, u32[]{:S(2)}) copy-start(f32[768,768]{1,0:T(8,128)} %param.7) | copy-start | bytes 7077892
  6.5 1.9 copy-start.4
  6.5 141.5 %reduce-scatter.2.cloned.1.call-start = ((), (), s32[]{:S(2)}) async-start(), calls=%async_computation.1 | async-start | bytes 3538944 | tf_op jit(solution)/shard_map/reduce_scatter | solution.py:59
  24.2 577.1 %all-reduce.7.cloned.1.call-start = ((), (), s32[]{:S(2)}) async-start(), calls=%async_computation.3 | async-start | bytes 4718592 | tf_op jit(solution)/shard_map/psum | solution.py:13
  151.0 0.7 copy-start.3
  151.0 741.3 %all-reduce.5.cloned.1.call-start = ((), (), s32[]{:S(2)}) async-start(), calls=%async_computation.2 | async-start | bytes 2359296 | tf_op jit(solution)/shard_map/psum | solution.py:13
  609.1 1.4 copy-start.1
  610.6 281.8 %copy-start.2 = (f32[768,384]{1,0:T(8,128)S(1)}, f32[768,384]{1,0:T(8,128)}, u32[]{:S(2)}) copy-start(f32[768,384]{1,0:T(8,128)} %reduce-scatter.2.cloned.1.call-done) | copy-start | bytes 3538948
Sparse Core Ops, SparseCore 0:
  24.3 123.7 reduce-scatter.1
  151.1 450.0 all-reduce.6
  611.8 280.4 all-reduce.4
where the time goes:
time: 906 us
  waiting for transfers between devices  849 us (94%)
  matrix products  22 us (2%)
  local copies, waits for them, and re-layouts  17.2 us (2%)
  between operations  13.2 us (1%)
    psum x2, waiting for transfers between devices, broadcast(): return lax.psum(block, axis)  725 us
    reduce_scatter x1, waiting for transfers between devices, local(): lax.psum_scatter(own_terms, 'half', scatter_dimension=0, tiled=True)  124 us
  transfers between devices with their start and end apart: 3, of which 3 were waited for; matrix products, arithmetic and copies ran while one was open for 1% of the time, Pallas kernels for 0%

commit v1 on v0

v1 whole, which is shorter than its diff:
```python
import jax
import jax.numpy as jnp
from jax import lax
from jax.experimental import pallas as pl
from jax.experimental.pallas import tpu as pltpu
from jax.sharding import PartitionSpec as P

BLK = 128
P_SIZE = 768
NF = 12288
MESH = pl.DeviceIdType.MESH


def move_kernel(child, slab_out, col_out, other_out, slab, col, cross, relay, other,
                slab_rx, col_rx, cross_rx, relay_rx, other_rx, tx, loc):
    half = lax.axis_index("half")
    row = lax.axis_index("row")
    colix = lax.axis_index("col")
    y, core = row // 2, row % 2
    x, z = colix // 8, colix % 8
    zz = half * 8 + z

    def at_x(step):
        return (half, row, ((x + step) % 4) * 8 + z)

    def at_z(step):
        return (half, row, x * 8 + (z + step + 8) % 8)

    def at_ring(step):
        there = (zz + step + 16) % 16
        return (there // 8, row, x * 8 + there % 8)

    def at_y(step):
        return (half, ((y + step) % 4) * 2 + core, colix)

    flip = (1 - half, row, colix)
    partner = (half, y * 2 + 1 - core, colix)

    barrier = pltpu.get_barrier_semaphore()
    peers = [at_x(1), at_x(2), at_x(3), at_z(1), at_z(-1), flip, at_ring(4), at_ring(-4),
             at_y(1), at_y(2), at_y(3), partner]
    for peer in peers:
        pl.semaphore_signal(barrier, inc=1, device_id=peer, device_id_type=MESH)
    pl.semaphore_wait(barrier, len(peers))

    pending = []
    count = [0]

    def send(src, dst, rx, device, when=None):
        copy = pltpu.make_async_remote_copy(
            src_ref=src, dst_ref=dst, send_sem=tx.at[count[0]], recv_sem=rx,
            device_id=device, device_id_type=MESH)
        count[0] += 1
        if when is None:
            copy.start()
        else:
            pl.when(when)(copy.start)
        pending.append((copy, when))

    def wait_rx(dst, rx, when=None):
        copy = pltpu.make_async_copy(dst, dst, rx)
        if when is None:
            copy.wait()
        else:
            pl.when(when)(copy.wait)

    def local(src, dst, sem):
        copy = pltpu.make_async_copy(src, dst, sem)
        copy.start()
        return copy

    is_source = (x == 0) & (z < 2)
    is_entry = z < 2
    mine = half * 512
    theirs = (1 - half) * 512
    jz = jnp.minimum(z, 1)

    for q in (2, 1, 3):
        send(child.at[pl.ds(theirs + q * 128, 128)], cross, cross_rx, at_x(q), is_source)
        send(child.at[pl.ds(mine + q * 128, 128)], slab.at[half, jz, q], slab_rx.at[half, jz, q], at_x(q), is_source)

    @pl.when(is_source)
    def _():
        first = local(child.at[pl.ds(theirs, 128)], cross, loc.at[0])
        second = local(child.at[pl.ds(mine, 128)], slab.at[half, jz, 0], loc.at[1])
        first.wait()
        second.wait()

    send(child.at[pl.ds(theirs, 256)], relay.at[0], relay_rx.at[0], at_ring(4))
    send(child.at[pl.ds(theirs + 256, 256)], relay.at[1], relay_rx.at[1], at_ring(-4))

    wait_rx(cross, cross_rx, is_entry & (x > 0))
    send(cross, slab.at[half, jz, x], slab_rx.at[half, jz, x], flip, is_entry)

    def own_piece(k, j, own):
        piece = slab.at[k, j, x]
        rx = slab_rx.at[k, j, x]
        if own:
            wait_rx(piece, rx, (z != j) | (x > 0))
        else:
            wait_rx(piece, rx)
        send(piece, piece, rx, at_z(1), (z >= j) & (z < 7))
        if j == 1:
            send(piece, piece, rx, at_z(-1), z == 1)
        send(piece, piece, rx, at_x(1))
        send(piece, piece, rx, at_x(3))

    for j in (0, 1):
        own_piece(half, j, True)
    for j in (0, 1):
        own_piece(1 - half, j, False)

    for leg, step in ((0, 4), (1, -4)):
        wait_rx(relay.at[leg], relay_rx.at[leg])
        send(relay.at[leg], other.at[leg], other_rx.at[leg], at_ring(step))

    left, right, far = (x + 3) % 4, (x + 1) % 4, (x + 2) % 4
    order = [(half, 0), (half, 1), (1 - half, 0), (1 - half, 1)]
    for k, j in order:
        wait_rx(slab.at[k, j, left], slab_rx.at[k, j, left])
        if j == 0:
            send(slab.at[k, j, left], slab.at[k, j, left], slab_rx.at[k, j, left], at_x(1))
        wait_rx(slab.at[k, j, right], slab_rx.at[k, j, right])
        if j == 1:
            send(slab.at[k, j, right], slab.at[k, j, right], slab_rx.at[k, j, right], at_x(3))
    for k, j in order:
        wait_rx(slab.at[k, j, far], slab_rx.at[k, j, far])

    holder = half == (z // 2) % 2
    lane = core == z // 4
    owner = holder & lane & (y == x)

    @pl.when(owner)
    def _():
        copies = [local(slab.at[m // 2, m % 2, pl.ds(2 * (z % 2), 2)], col.at[m], loc.at[m]) for m in range(4)]
        for copy in copies:
            copy.wait()

    for step in (2, 1, 3):
        to = (y + step) % 4
        send(col.at[to], col.at[to], col_rx.at[to], at_y(step), owner)
    wait_rx(col.at[y], col_rx.at[y], lane & jnp.logical_not(owner))
    send(col.at[y], col.at[y], col_rx.at[y], flip, holder & lane)
    for step in (2, 1, 3):
        to = (y + step) % 4
        send(col.at[y], col.at[y], col_rx.at[y], at_y(step), lane & jnp.logical_not(holder & (to == x)))
    send(col.at[y], col.at[y], col_rx.at[y], partner, lane)
    for step in (1, 3, 2):
        m = (y + step) % 4
        wait_rx(col.at[m], col_rx.at[m], lane & jnp.logical_not(owner))
        send(col.at[m], col.at[m], col_rx.at[m], partner, lane)
    for m in range(4):
        wait_rx(col.at[m], col_rx.at[m], jnp.logical_not(lane))

    outs = [local(slab, slab_out, loc.at[0]), local(col, col_out, loc.at[1])]
    for leg in (0, 1):
        wait_rx(other.at[leg], other_rx.at[leg])
    outs.append(local(other, other_out, loc.at[2]))
    for copy in outs:
        copy.wait()
    for copy, when in pending:
        if when is None:
            copy.wait_send()
        else:
            pl.when(when)(copy.wait_send)


def move(child_tile):
    f32 = jnp.float32
    any_spec = pl.BlockSpec(memory_space=pl.ANY)
    return pl.pallas_call(
        move_kernel,
        out_shape=(jax.ShapeDtypeStruct((2, 2, 4, 128, 256), f32),
                   jax.ShapeDtypeStruct((4, 2, 128, 256), f32),
                   jax.ShapeDtypeStruct((2, 256, 256), f32)),
        in_specs=[any_spec],
        out_specs=(any_spec, any_spec, any_spec),
        scratch_shapes=[
            pltpu.VMEM((2, 2, 4, 128, 256), f32),
            pltpu.VMEM((4, 2, 128, 256), f32),
            pltpu.VMEM((128, 256), f32),
            pltpu.VMEM((2, 256, 256), f32),
            pltpu.VMEM((2, 256, 256), f32),
            pltpu.SemaphoreType.DMA((2, 2, 4)),
            pltpu.SemaphoreType.DMA((4,)),
            pltpu.SemaphoreType.DMA,
            pltpu.SemaphoreType.DMA((2,)),
            pltpu.SemaphoreType.DMA((2,)),
            pltpu.SemaphoreType.DMA((48,)),
            pltpu.SemaphoreType.DMA((4,)),
        ],
        compiler_params=pltpu.CompilerParams(collective_id=0, has_side_effects=True),
    )(child_tile)


def expand_rows(tile, places):
    triples = tile.shape[0] // (2 * BLK)
    pairs = tile.reshape(triples, 2, BLK, tile.shape[1])
    first, second = pairs[:, 0], pairs[:, 1]
    where_first = places[0::2][:, None, None]
    where_second = places[1::2][:, None, None]
    zero = jnp.zeros((), tile.dtype)
    top = jnp.where(where_first == 0, first, zero)
    middle = jnp.where(where_first == 1, first, jnp.where(where_second == 1, second, zero))
    bottom = jnp.where(where_second == 2, second, zero)
    return jnp.stack([top, middle, bottom], axis=1).reshape(triples * 3 * BLK, tile.shape[1])


def expand_cols(tile, places):
    first, second = tile[:, :BLK], tile[:, BLK:]
    zero = jnp.zeros((), tile.dtype)
    return jnp.concatenate([
        jnp.where(places[0] == 0, first, zero),
        jnp.where(places[0] == 1, first, jnp.where(places[1] == 1, second, zero)),
        jnp.where(places[1] == 2, second, zero),
    ], axis=1)


def local(child_updates, child_maps, panel_pattern, pivot_inverse):
    child_tile = child_updates[0]
    half_index = lax.axis_index("half")
    row_index = lax.axis_index("row")
    col_index = lax.axis_index("col")
    slab, col, other = move(child_tile)
    slab_index = 2 * row_index + half_index
    places = child_maps - 3 * (jnp.arange(64, dtype=jnp.int32) // 2)[None, :]
    slab_places = lax.dynamic_slice(places, (0, 4 * slab_index), (2, 4))
    col_places = lax.dynamic_slice(places, (0, 2 * col_index), (2, 2))

    own_rows = lax.dynamic_slice_in_dim(child_tile, half_index * 512, 512, 0)
    other_rows = other.reshape(512, 256)
    first_rows = jnp.where(half_index == 0, own_rows, other_rows)
    second_rows = jnp.where(half_index == 0, other_rows, own_rows)
    assembled = sum(
        expand_cols(expand_rows(t, slab_places[k]), col_places[k])
        for k, t in ((0, first_rows), (1, second_rows)))

    def panel(raw, row_places):
        return jnp.concatenate([
            sum(expand_cols(expand_rows(raw[k][j], row_places[k]), places[k, 2 * j:2 * j + 2]) for k in (0, 1))
            for j in (0, 1)], axis=1)

    slab_panel = panel([[slab[k, j].reshape(512, 256) for j in (0, 1)] for k in (0, 1)], slab_places)
    col_panel = panel([[col[2 * k + j].reshape(256, 256) for j in (0, 1)] for k in (0, 1)], col_places)

    def factor_of(rows, block0, blocks):
        pattern = lax.dynamic_slice_in_dim(panel_pattern, block0, blocks, 0)
        mask = jnp.repeat(jnp.repeat(pattern, BLK, axis=0), BLK, axis=1).astype(jnp.float32)
        return lax.dot_general(rows, pivot_inverse, (((1,), (1,)), ((), ())), precision=lax.Precision.HIGH) * mask

    factor = factor_of(slab_panel, slab_index * 6, 6)
    col_factor = factor_of(col_panel, col_index * 3, 3)
    schur = lax.dot_general(factor, col_factor, (((1,), (1,)), ((), ())), precision=lax.Precision.HIGH)
    pivots = jnp.where(col_index == 0, factor[:, :384], factor[:, 384:])
    result = jnp.where(col_index < 2, pivots, jnp.where(slab_index == 0, assembled, assembled - schur))
    return result.reshape(1, 1, 768, 384)


def solution(mesh):
    placed = (P("half", "row", "col"), P(), P(), P())
    return jax.shard_map(
        local, mesh=mesh, in_specs=placed, out_specs=P("row", "half", None, "col"), check_vma=False
    )
```

time: 906 us -> 200 us (0.22)
  the two profiles are of different devices: /device:TPU:1 before, /device:TPU:224 now
where the time goes in v1:
time: 200 us
  Pallas kernels  143 us (72%)
  between operations  15.7 us (8%)
  local copies, waits for them, and re-layouts  15.3 us (8%)
  matrix products  13.7 us (7%)
  other arithmetic  12.5 us (6%)
    pallas_call x1, Pallas kernels, move(): pl.pallas_call(move_kernel, out_shape=(jax.ShapeDtypeStruct((2, 2, 4, 128...  143 us
    dot_general x2, matrix products, factor_of(): lax.dot_general(rows, pivot_inverse, (((1,), (1,)), ((), ())), precision=...  7.58 us
    dot_general x1, matrix products, local(): lax.dot_general(factor, col_factor, (((1,), (1,)), ((), ())), precision=l...  6.13 us
    select_n x3, other arithmetic, expand_rows(): top = jnp.where(where_first == 0, first, zero)  5.73 us
    unnamed x46, local copies, waits for them, and re-layouts  4.89 us

profile of v1, /device:TPU:224, one launch (start us, length us, event | category | flops | bytes accessed | tf_op | source)
XLA Modules:
  0.0 199.8 jit_solution(1544136606411886583)
XLA Ops:
  0.0 0.9 dynamic-slice_convert_fusion.1
  1.0 1.6 broadcast_in_dim.280
  2.6 3.1 %copy.7 = f32[768,768]{1,0:T(8,128)} copy(f32[768,768]{0,1:T(8,128)} %bitcast.67) | data formatting | bytes 4718592 | tf_op jit(solution)/shard_map/convert_element_type | solution.py:248
  5.7 142.6 %shard_map.46 = (f32[2,2,4,128,256]{4,3,2,1,0:T(8,128)}, f32[4,2,128,256]{3,2,1,0:T(8,128)}, f32[2,256,256]{2,1,0:T(8,128)}) custom-call(f32[1024,256]{1,0:T(8,128)} %bitcast.75), custom_call_target="tpu_custom_call" | custom-call | tf_op jit(solution)/shard_map/pallas_call | solution.py:171
  148.3 3.0 %fusion.15 = (f32[1,1,4,128,256]{4,3,2,1,0:T(8,128)}, f32[1,1,4,128,256]{4,3,2,1,0:T(8,128)}, f32[1,1,4,128,256]{4,3,2,1,0:T(8,128)}, f32[1,1,4,128,256]{4,3,2,1,0:T(8,128)}) fusion(f32[2,2,4,128,256]{4,3,2,1,0:T(8,128)} %get-tuple-element.8), kind=kLoop, calls=%fused_computation.117 | loop fusion | bytes 4194304 | tf_op jit(solution)/shard_map/slice | solution.py:243
  151.4 0.1 slice.314
  151.5 0.1 slice.304
  151.6 0.1 slice.307
  151.7 0.8 constant_dynamic-slice_fusion
  152.5 1.3 broadcast_select_fusion
  153.9 2.3 %slice_select_fusion.20 = (f32[2,1,128,256]{3,2,1,0:T(8,128)S(1)}, f32[2,1,128,256]{3,2,1,0:T(8,128)S(1)}, f32[2,1,128,256]{3,2,1,0:T(8,128)S(1)}, f32[2,1,128,2...) fusion(f32[2,2,128,256]{3,2,1,0:T(8,128)S(1)} %bitcast.79, ...), kind=kLoop, calls=%fused_computation.61 | loop fusion | flops 786432 | bytes 3932168 | tf_op jit(solution)/shard_map/jit(_where)/select_n | solution.py:203
  156.2 0.7 fusion.17
  159.5 1.1 slice_select_fusion.8
  160.6 0.1 slice.317
  160.7 2.1 %slice_select_fusion.18 = (f32[2,1,128,256]{3,2,1,0:T(8,128)S(1)}, f32[2,1,128,256]{3,2,1,0:T(8,128)S(1)}, f32[2,1,128,256]{3,2,1,0:T(8,128)S(1)}, f32[2,1,128,2...) fusion(f32[2,2,128,256]{3,2,1,0:T(8,128)} %bitcast.78, ...), kind=kLoop, calls=%fused_computation.59 | loop fusion | flops 786432 | bytes 3932168 | tf_op jit(solution)/shard_map/jit(_where)/select_n | solution.py:203
  165.5 0.1 slice_select_fusion.6
  165.6 0.1 maximum_add_fusion.1
  165.7 0.8 copy-done.16
  169.1 0.1 slice_select_fusion.12
  172.0 0.1 maximum_add_fusion
  172.1 1.5 copy-done.1
  173.7 4.6 %fusion.4 = f32[768,768]{1,0:T(8,128)} fusion(f32[768,768]{1,0:T(8,128)S(1)} %copy-done.1, f32[768,768]{1,0:T(8,128)S(1)} %copy-done, f32[768,384]{1,0:T(8,128)S(1)} %maximum_add_fusion.1, f32[768,384]{1,0:T(8,128)S(1)} %maximum_add_fusion), kind=kOutput, calls=%fused_computation.5 | convolution fusion | flops 2719088640 | bytes 9437184 | tf_op jit(solution)/shard_map/dot_general | solution.py:249
  178.5 0.6 fusion.16
  184.2 1.4 slice_select_fusion.38
  185.8 1.1 copy-done.6
  187.2 3.0 %convolution_multiply_fusion = f32[384,768]{0,1:T(8,128)} fusion(f32[384,768]{0,1:T(8,128)S(1)} %bitcast.68, f32[768,768]{1,0:T(8,128)S(1)} %copy-done, f32[384,384]{1,0:T(8,128)S(1)} %maximum_add_fusion.4, f32[384,384]{1,0:T(8,128)S(1)} %maximum_add_fusion.3), kind=kOutput, calls=%fused_computation.6 | convolution fusion | flops 1359544320 | bytes 5898240 | tf_op jit(solution)/shard_map/dot_general | solution.py:249
  190.4 1.1 slice_select_fusion.4
  191.4 0.1 copy-done.14
  191.6 0.3 copy-done.15
  192.0 1.1 slice_select_fusion.2
  193.0 0.6 copy-done.2
  193.7 6.1 %fusion.8 = f32[1,1,768,384]{3,2,1,0:T(8,128)} fusion(f32[768,768]{1,0:T(8,128)} %fusion.4, f32[384,768]{0,1:T(8,128)S(1)} %copy-done.2, f32[768,128]{1,0:T(8,128)} %get-tuple-element.33, f32[768,128]{1,0:T(8,128)} %get-tuple-element.34, f32[768,128]{1,0:T(8,128)} %get-tuple-element.32, f32[768,128]{1,0:T(8,128)} %get-tuple-element.30, ...), kind=kOutput, calls=%fused_computation.8 | convolution fusion | flops 1361608704 | bytes 9437187 | tf_op jit(solution)/shard_map/dot_general | solution.py:253
  (66 shorter events, 1.7 us)
Async XLA Ops:
  0.0 172.1 %copy-start = (f32[768,768]{1,0:T(8,128)S(1)}, f32[768,768]{1,0:T(8,128)}, u32[]{:S(2)}) copy-start(f32[768,768]{1,0:T(8,128)} %param.7) | copy-start | bytes 7077892
  148.3 3.0 %copy-start.20 = (s32[2,64]{1,0:T(2,128)S(1)}, s32[2,64]{1,0:T(2,128)}, u32[]{:S(2)}) copy-start(s32[2,64]{1,0:T(2,128)} %param.5) | copy-start | bytes 1540
  148.3 3.4 %copy-start.3 = (f32[1,1024,256]{2,1,0:T(8,128)S(1)}, f32[1,1024,256]{2,1,0:T(8,128)}, u32[]{:S(2)}) copy-start(f32[1,1024,256]{2,1,0:T(8,128)} %param.4) | copy-start | bytes 3145732
  152.5 1.4 copy-start.5
  156.2 4.5 %copy-start.4 = (f32[1,1,4,128,256]{4,3,2,1,0:T(8,128)S(1)}, f32[1,1,4,128,256]{4,3,2,1,0:T(8,128)}, u32[]{:S(2)}) copy-start(f32[1,1,4,128,256]{4,3,2,1,0:T(8,128)} %get-tuple-element.11) | copy-start | bytes 1572868
  162.8 2.8 %copy-start.7 = (f32[768,128]{1,0:T(8,128)S(1)}, f32[768,128]{1,0:T(8,128)}, u32[]{:S(2)}) copy-start(f32[768,128]{1,0:T(8,128)} %get-tuple-element.44) | copy-start | bytes 1179652
  162.8 2.8 %copy-start.8 = (f32[768,128]{1,0:T(8,128)S(1)}, f32[768,128]{1,0:T(8,128)}, u32[]{:S(2)}) copy-start(f32[768,128]{1,0:T(8,128)} %get-tuple-element.45) | copy-start | bytes 1179652
  162.8 2.8 %copy-start.9 = (f32[768,128]{1,0:T(8,128)S(1)}, f32[768,128]{1,0:T(8,128)}, u32[]{:S(2)}) copy-start(f32[768,128]{1,0:T(8,128)} %get-tuple-element.46) | copy-start | bytes 1179652
  165.6 1.0 copy-start.16
  165.6 1.0 copy-start.17
  165.6 1.1 copy-start.18
  172.0 1.7 copy-start.1
  173.7 4.6 %copy-start.19 = (s32[96,6]{0,1:T(8,128)S(1)}, s32[96,6]{0,1:T(8,128)}, u32[]{:S(2)}) copy-start(s32[96,6]{0,1:T(8,128)} %param.6) | copy-start | bytes 6916
  185.7 1.2 copy-start.6
  187.2 3.1 %copy-start.10 = (f32[2,1,128,256]{3,2,1,0:T(8,128)S(1)}, f32[2,1,128,256]{3,2,1,0:T(8,128)}, u32[]{:S(2)}) copy-start(f32[2,1,128,256]{3,2,1,0:T(8,128)} %get-tuple-element.77) | copy-start | bytes 786436
  187.2 3.0 %copy-start.11 = (f32[2,1,128,256]{3,2,1,0:T(8,128)S(1)}, f32[2,1,128,256]{3,2,1,0:T(8,128)}, u32[]{:S(2)}) copy-start(f32[2,1,128,256]{3,2,1,0:T(8,128)} %get-tuple-element.78) | copy-start | bytes 786436
  187.2 3.0 %copy-start.12 = (f32[2,1,128,256]{3,2,1,0:T(8,128)S(1)}, f32[2,1,128,256]{3,2,1,0:T(8,128)}, u32[]{:S(2)}) copy-start(f32[2,1,128,256]{3,2,1,0:T(8,128)} %get-tuple-element.79) | copy-start | bytes 786436
  190.4 1.1 copy-start.13
  190.4 1.2 copy-start.14
  190.4 1.5 copy-start.15
  192.0 1.7 copy-start.2

commit v2 on v1

--- a/solution.py
+++ b/solution.py
@@ -193,66 +193,118 @@
     )(child_tile)
 
 
-def expand_rows(tile, places):
-    triples = tile.shape[0] // (2 * BLK)
-    pairs = tile.reshape(triples, 2, BLK, tile.shape[1])
-    first, second = pairs[:, 0], pairs[:, 1]
-    where_first = places[0::2][:, None, None]
-    where_second = places[1::2][:, None, None]
-    zero = jnp.zeros((), tile.dtype)
-    top = jnp.where(where_first == 0, first, zero)
-    middle = jnp.where(where_first == 1, first, jnp.where(where_second == 1, second, zero))
-    bottom = jnp.where(where_second == 2, second, zero)
-    return jnp.stack([top, middle, bottom], axis=1).reshape(triples * 3 * BLK, tile.shape[1])
-
-
-def expand_cols(tile, places):
-    first, second = tile[:, :BLK], tile[:, BLK:]
-    zero = jnp.zeros((), tile.dtype)
-    return jnp.concatenate([
-        jnp.where(places[0] == 0, first, zero),
-        jnp.where(places[0] == 1, first, jnp.where(places[1] == 1, second, zero)),
-        jnp.where(places[1] == 2, second, zero),
-    ], axis=1)
+def split(value):
+    high = value.astype(jnp.bfloat16)
+    return high, (value - high.astype(jnp.float32)).astype(jnp.bfloat16)
+
+
+def dot3(a_high, a_low, b_high, b_low):
+    def dot(a, b):
+        return lax.dot_general(a, b, (((1,), (1,)), ((), ())), preferred_element_type=jnp.float32)
+    return dot(a_high, b_high) + (dot(a_high, b_low) + dot(a_low, b_high))
+
+
+def weights(maps, k, triple):
+    first = maps[k, 2 * triple] - 3 * triple
+    second = maps[k, 2 * triple + 1] - 3 * triple
+    return [jnp.where(t, 1.0, 0.0).astype(jnp.float32) for t in (first == 0, first == 1, second == 1, second == 2)]
+
+
+def expand(pairs, row_weights, col_weights):
+    total = [[None] * 3 for _ in range(3)]
+    for (first, second), rw, cw in zip(pairs, row_weights, col_weights):
+        rows = (first * rw[0], first * rw[1] + second * rw[2], second * rw[3])
+        for p, value in enumerate(rows):
+            left, right = value[:, :BLK], value[:, BLK:]
+            for q, part in enumerate((left * cw[0], left * cw[1] + right * cw[2], right * cw[3])):
+                total[p][q] = part if total[p][q] is None else total[p][q] + part
+    return total
+
+
+def front_kernel(maps, pattern, inverse, child, other, slab, col, out,
+                 inv_high, inv_low, tile_high, tile_low, fac_high, fac_low):
+    half = lax.axis_index("half")
+    row = lax.axis_index("row")
+    colix = lax.axis_index("col")
+    slab_index = 2 * row + half
+    for b in range(6):
+        rows = slice(b * BLK, (b + 1) * BLK)
+        inv_high[rows], inv_low[rows] = split(inverse[rows])
+    panel_cols = [[weights(maps, k, j) for k in (0, 1)] for j in (0, 1)]
+    for t in range(3):
+        triple = 2 * slab_index + t if t < 2 else colix
+        row_weights = [weights(maps, k, triple) for k in (0, 1)]
+        for j in range(2):
+            if t < 2:
+                pairs = [(slab[k, j, 2 * t], slab[k, j, 2 * t + 1]) for k in (0, 1)]
+            else:
+                pairs = [(col[2 * k + j, 0], col[2 * k + j, 1]) for k in (0, 1)]
+            blocks = expand(pairs, row_weights, panel_cols[j])
+            for p in range(3):
+                for q in range(3):
+                    high, low = split(blocks[p][q])
+                    where = (slice(p * BLK, (p + 1) * BLK), slice((3 * j + q) * BLK, (3 * j + q + 1) * BLK))
+                    tile_high[t, where[0], where[1]] = high
+                    tile_low[t, where[0], where[1]] = low
+        for n in range(3):
+            depth = (n + 1) * 256
+            cols = slice(n * 256, depth)
+            product = dot3(tile_high[t, :, :depth], tile_low[t, :, :depth],
+                           inv_high[cols, :depth], inv_low[cols, :depth])
+            for p in range(3):
+                for q in range(2):
+                    b = 2 * n + q
+                    block = product[p * BLK:(p + 1) * BLK, q * BLK:(q + 1) * BLK]
+                    block = block * pattern[3 * triple + p, b].astype(jnp.float32)
+                    rows = slice(t * 384 + p * BLK, t * 384 + (p + 1) * BLK)
+                    high, low = split(block)
+                    fac_high[rows, b * BLK:(b + 1) * BLK] = high
+                    fac_low[rows, b * BLK:(b + 1) * BLK] = low
+                    if t < 2:
+                        @pl.when(colix == b // 3)
+                        def _(rows=rows, b=b, block=block):
+                            out[rows, (b % 3) * BLK:(b % 3 + 1) * BLK] = block
+
+    @pl.when(colix >= 2)
+    def _():
+        col_weights = [weights(maps, k, colix) for k in (0, 1)]
+        keep = slab_index == 0
+        for t in range(2):
+            schur = dot3(fac_high[t * 384:(t + 1) * 384], fac_low[t * 384:(t + 1) * 384],
+                         fac_high[768:], fac_low[768:])
+            row_weights = [weights(maps, k, 2 * slab_index + t) for k in (0, 1)]
+            own = [child[pl.ds(half * 512 + t * 256 + i * BLK, BLK), :] for i in (0, 1)]
+            sent = [other[t, i * BLK:(i + 1) * BLK, :] for i in (0, 1)]
+            ordered = [[jnp.where(half == k, a, b) for a, b in zip(own, sent)] for k in (0, 1)]
+            blocks = expand(ordered, row_weights, col_weights)
+            for p in range(3):
+                for q in range(3):
+                    term = schur[p * BLK:(p + 1) * BLK, q * BLK:(q + 1) * BLK]
+                    out[t * 384 + p * BLK:t * 384 + (p + 1) * BLK, q * BLK:(q + 1) * BLK] = (
+                        blocks[p][q] - jnp.where(keep, 0.0, term))
 
 
 def local(child_updates, child_maps, panel_pattern, pivot_inverse):
     child_tile = child_updates[0]
-    half_index = lax.axis_index("half")
-    row_index = lax.axis_index("row")
-    col_index = lax.axis_index("col")
     slab, col, other = move(child_tile)
-    slab_index = 2 * row_index + half_index
-    places = child_maps - 3 * (jnp.arange(64, dtype=jnp.int32) // 2)[None, :]
-    slab_places = lax.dynamic_slice(places, (0, 4 * slab_index), (2, 4))
-    col_places = lax.dynamic_slice(places, (0, 2 * col_index), (2, 2))
-
-    own_rows = lax.dynamic_slice_in_dim(child_tile, half_index * 512, 512, 0)
-    other_rows = other.reshape(512, 256)
-    first_rows = jnp.where(half_index == 0, own_rows, other_rows)
-    second_rows = jnp.where(half_index == 0, other_rows, own_rows)
-    assembled = sum(
-        expand_cols(expand_rows(t, slab_places[k]), col_places[k])
-        for k, t in ((0, first_rows), (1, second_rows)))
-
-    def panel(raw, row_places):
-        return jnp.concatenate([
-            sum(expand_cols(expand_rows(raw[k][j], row_places[k]), places[k, 2 * j:2 * j + 2]) for k in (0, 1))
-            for j in (0, 1)], axis=1)
-
-    slab_panel = panel([[slab[k, j].reshape(512, 256) for j in (0, 1)] for k in (0, 1)], slab_places)
-    col_panel = panel([[col[2 * k + j].reshape(256, 256) for j in (0, 1)] for k in (0, 1)], col_places)
-
-    def factor_of(rows, block0, blocks):
-        pattern = lax.dynamic_slice_in_dim(panel_pattern, block0, blocks, 0)
-        mask = jnp.repeat(jnp.repeat(pattern, BLK, axis=0), BLK, axis=1).astype(jnp.float32)
-        return lax.dot_general(rows, pivot_inverse, (((1,), (1,)), ((), ())), precision=lax.Precision.HIGH) * mask
-
-    factor = factor_of(slab_panel, slab_index * 6, 6)
-    col_factor = factor_of(col_panel, col_index * 3, 3)
-    schur = lax.dot_general(factor, col_factor, (((1,), (1,)), ((), ())), precision=lax.Precision.HIGH)
-    pivots = jnp.where(col_index == 0, factor[:, :384], factor[:, 384:])
-    result = jnp.where(col_index < 2, pivots, jnp.where(slab_index == 0, assembled, assembled - schur))
+    smem = pl.BlockSpec(memory_space=pltpu.SMEM)
+    vmem = pl.BlockSpec(memory_space=pltpu.VMEM)
+    bf16 = jnp.bfloat16
+    result = pl.pallas_call(
+        front_kernel,
+        out_shape=jax.ShapeDtypeStruct((768, 384), jnp.float32),
+        in_specs=[smem, smem] + [vmem] * 5,
+        out_specs=vmem,
+        scratch_shapes=[
+            pltpu.VMEM((768, 768), bf16),
+            pltpu.VMEM((768, 768), bf16),
+            pltpu.VMEM((3, 384, 768), bf16),
+            pltpu.VMEM((3, 384, 768), bf16),
+            pltpu.VMEM((1152, 768), bf16),
+            pltpu.VMEM((1152, 768), bf16),
+        ],
+        compiler_params=pltpu.CompilerParams(vmem_limit_bytes=48 * 2**20),
+    )(child_maps, panel_pattern, pivot_inverse, child_tile, other, slab, col)
     return result.reshape(1, 1, 768, 384)
 
 

time: 200 us -> 162 us (0.81)
  between operations: 15.7 us -> 0.02 us
  matrix products: 13.7 us -> 0 us
  other arithmetic: 12.5 us -> 0 us
  Pallas kernels: 143 us -> 155 us
  local copies, waits for them, and re-layouts: 15.3 us -> 6.54 us
    dot_general x3 -> x0, matrix products: 13.7 us -> none  [the longest x2 7.58 us: factor_of(): lax.dot_general(rows, pivot_inverse, (((1,), (1,)), ((), ())), precision=...]
    pallas_call x0 -> x1, Pallas kernels: none -> 12.4 us  [local(): pl.pallas_call(front_kernel, out_shape=jax.ShapeDtypeStruct((768, 384), j...]
    select_n x15 -> x0, other arithmetic: 10.7 us -> none  [the longest x3 5.73 us: expand_rows(): top = jnp.where(where_first == 0, first, zero)]
    slice x7 -> x0, local copies, waits for them, and re-layouts: 4.63 us -> none  [the longest x1 2.97 us: local(): slab[k, j].reshape(512, 256)]
    convert_element_type x1 -> x0, local copies, waits for them, and re-layouts: 3.08 us -> none  [factor_of(): jnp.repeat(jnp.repeat(pattern, BLK, axis=0), BLK, axis=1)]
    unnamed x46 -> x11, local copies, waits for them, and re-layouts: 4.89 us -> 6.54 us
where the time goes in v2:
time: 162 us; the launch traced here: 161 us
  Pallas kernels  155 us (96%)
  local copies, waits for them, and re-layouts  6.54 us (4%)
    pallas_call x1, Pallas kernels, move(): pl.pallas_call(move_kernel, out_shape=(jax.ShapeDtypeStruct((2, 2, 4, 128...  143 us
    pallas_call x1, Pallas kernels, local(): pl.pallas_call(front_kernel, out_shape=jax.ShapeDtypeStruct((768, 384), j...  12.4 us
    unnamed x11, local copies, waits for them, and re-layouts  6.54 us

profile of v2, /device:TPU:224, one launch (start us, length us, event | category | flops | bytes accessed | tf_op | source)
XLA Modules:
  0.0 161.5 jit_solution(15719010024965282919)
XLA Ops:
  0.0 0.8 copy.5.pattern
  0.8 142.5 %shard_map.46 = (f32[2,2,4,128,256]{4,3,2,1,0:T(8,128)}, f32[4,2,128,256]{3,2,1,0:T(8,128)}, f32[2,256,256]{2,1,0:T(8,128)}) custom-call(f32[1024,256]{1,0:T(8,128)} %bitcast.2), custom_call_target="tpu_custom_call" | custom-call | tf_op jit(solution)/shard_map/pallas_call | solution.py:171
  143.3 0.0 copy-start
  143.3 1.2 copy-done
  144.6 0.0 copy-start.1
  144.6 1.6 copy-done.1
  146.2 0.0 copy-start.2
  146.2 1.2 copy-done.2
  147.4 0.0 copy-start.3
  147.4 1.0 copy-done.3
  148.4 0.0 copy-start.4
  148.4 0.7 copy-done.4
  149.1 12.4 %shard_map.47 = f32[768,384]{1,0:T(8,128)} custom-call(s32[2,64]{1,0:T(2,128)S(1)} %copy-done.4, s32[96,6]{1,0:T(8,128)S(1)} %copy.5.pattern, f32[768,768]{1,0:T(8,128)} %inverse.1, f32[1024,256]{1,0:T(8,128)S(1)} %bitcast.3, f32[2,256,256]{2,1,0:T(8,128)S(1)} %copy-done.3, f32[2,2,4,128,256]{4,3,2,1,0:T(8,128)S(1)} %copy-done.1, ...), custom_call_target="tpu_custom_call" | custom-call | tf_op jit(solution)/shard_map/pallas_call | solution.py:293
Async XLA Ops:
  143.3 1.2 copy-start
  144.6 1.6 copy-start.1
  146.2 1.2 copy-start.2
  147.4 1.0 copy-start.3
  148.4 0.7 copy-start.4

commit v3 on v2

--- a/solution.py
+++ b/solution.py
@@ -9,16 +9,17 @@
 P_SIZE = 768
 NF = 12288
 MESH = pl.DeviceIdType.MESH
-
-
-def move_kernel(child, slab_out, col_out, other_out, slab, col, cross, relay, other,
-                slab_rx, col_rx, cross_rx, relay_rx, other_rx, tx, loc):
+PARTS = 2
+LAG = 2
+
+
+def move_kernel(child, slab_out, col_out, other_out, slab, col, cross, other,
+                slab_rx, col_rx, cross_rx, other_rx, tx, loc, cross_loc):
     half = lax.axis_index("half")
     row = lax.axis_index("row")
     colix = lax.axis_index("col")
     y, core = row // 2, row % 2
     x, z = colix // 8, colix % 8
-    zz = half * 8 + z
 
     def at_x(step):
         return (half, row, ((x + step) % 4) * 8 + z)
@@ -26,10 +27,6 @@
     def at_z(step):
         return (half, row, x * 8 + (z + step + 8) % 8)
 
-    def at_ring(step):
-        there = (zz + step + 16) % 16
-        return (there // 8, row, x * 8 + there % 8)
-
     def at_y(step):
         return (half, ((y + step) % 4) * 2 + core, colix)
 
@@ -37,7 +34,7 @@
     partner = (half, y * 2 + 1 - core, colix)
 
     barrier = pltpu.get_barrier_semaphore()
-    peers = [at_x(1), at_x(2), at_x(3), at_z(1), at_z(-1), flip, at_ring(4), at_ring(-4),
+    peers = [at_x(1), at_x(2), at_x(3), at_z(1), at_z(-1), flip,
              at_y(1), at_y(2), at_y(3), partner]
     for peer in peers:
         pl.semaphore_signal(barrier, inc=1, device_id=peer, device_id_type=MESH)
@@ -75,26 +72,36 @@
     theirs = (1 - half) * 512
     jz = jnp.minimum(z, 1)
 
-    for q in (2, 1, 3):
-        send(child.at[pl.ds(theirs + q * 128, 128)], cross, cross_rx, at_x(q), is_source)
-        send(child.at[pl.ds(mine + q * 128, 128)], slab.at[half, jz, q], slab_rx.at[half, jz, q], at_x(q), is_source)
+    part = BLK // PARTS
+
+    def rows_of(start, s):
+        return pl.ds(start + s * part, part)
+
+    for s in range(PARTS):
+        for q in (2, 1, 3):
+            send(child.at[rows_of(theirs + q * 128, s)], cross.at[s], cross_rx.at[s], at_x(q), is_source)
+            send(child.at[rows_of(mine + q * 128, s)], slab.at[half, jz, q, rows_of(0, s)],
+                 slab_rx.at[half, jz, q, s], at_x(q), is_source)
 
     @pl.when(is_source)
     def _():
-        first = local(child.at[pl.ds(theirs, 128)], cross, loc.at[0])
-        second = local(child.at[pl.ds(mine, 128)], slab.at[half, jz, 0], loc.at[1])
-        first.wait()
-        second.wait()
-
-    send(child.at[pl.ds(theirs, 256)], relay.at[0], relay_rx.at[0], at_ring(4))
-    send(child.at[pl.ds(theirs + 256, 256)], relay.at[1], relay_rx.at[1], at_ring(-4))
-
-    wait_rx(cross, cross_rx, is_entry & (x > 0))
-    send(cross, slab.at[half, jz, x], slab_rx.at[half, jz, x], flip, is_entry)
-
-    def own_piece(k, j, own):
-        piece = slab.at[k, j, x]
-        rx = slab_rx.at[k, j, x]
+        copies = [local(child.at[pl.ds(mine, 128)], slab.at[half, jz, 0], loc.at[0])]
+        copies += [local(child.at[rows_of(theirs, s)], cross.at[s], cross_loc.at[s]) for s in range(PARTS)]
+        for copy in copies:
+            copy.wait()
+
+    def exchange(i):
+        send(child.at[pl.ds(theirs + 64 * i, 64)], other.at[i], other_rx.at[i], flip)
+
+    exchange(0)
+    exchange(1)
+    left, right, far = (x + 3) % 4, (x + 1) % 4, (x + 2) % 4
+
+    def piece_of(k, j, q, s):
+        return slab.at[k, j, q, rows_of(0, s)], slab_rx.at[k, j, q, s]
+
+    def own_piece(k, j, s, own):
+        piece, rx = piece_of(k, j, x, s)
         if own:
             wait_rx(piece, rx, (z != j) | (x > 0))
         else:
@@ -105,26 +112,33 @@
         send(piece, piece, rx, at_x(1))
         send(piece, piece, rx, at_x(3))
 
-    for j in (0, 1):
-        own_piece(half, j, True)
-    for j in (0, 1):
-        own_piece(1 - half, j, False)
-
-    for leg, step in ((0, 4), (1, -4)):
-        wait_rx(relay.at[leg], relay_rx.at[leg])
-        send(relay.at[leg], other.at[leg], other_rx.at[leg], at_ring(step))
-
-    left, right, far = (x + 3) % 4, (x + 1) % 4, (x + 2) % 4
-    order = [(half, 0), (half, 1), (1 - half, 0), (1 - half, 1)]
-    for k, j in order:
-        wait_rx(slab.at[k, j, left], slab_rx.at[k, j, left])
+    def side_pieces(k, j, s):
+        piece, rx = piece_of(k, j, left, s)
+        wait_rx(piece, rx)
         if j == 0:
-            send(slab.at[k, j, left], slab.at[k, j, left], slab_rx.at[k, j, left], at_x(1))
-        wait_rx(slab.at[k, j, right], slab_rx.at[k, j, right])
+            send(piece, piece, rx, at_x(1))
+        piece, rx = piece_of(k, j, right, s)
+        wait_rx(piece, rx)
         if j == 1:
-            send(slab.at[k, j, right], slab.at[k, j, right], slab_rx.at[k, j, right], at_x(3))
-    for k, j in order:
-        wait_rx(slab.at[k, j, far], slab_rx.at[k, j, far])
+            send(piece, piece, rx, at_x(3))
+
+    for s in range(PARTS):
+        wait_rx(cross.at[s], cross_rx.at[s], is_entry & (x > 0))
+        piece, rx = piece_of(half, jz, x, s)
+        send(cross.at[s], piece, rx, flip, is_entry)
+    order = [(own, j, s) for own in (True, False) for s in range(PARTS) for j in (0, 1)]
+    for at, (own, j, s) in enumerate(order):
+        own_piece(half if own else 1 - half, j, s, own)
+        if at + 2 < 8:
+            exchange(at + 2)
+        if at >= LAG:
+            own, j, s = order[at - LAG]
+            side_pieces(half if own else 1 - half, j, s)
+    for own, j, s in order[len(order) - LAG:]:
+        side_pieces(half if own else 1 - half, j, s)
+    for own, j, s in order:
+        piece, rx = piece_of(half if own else 1 - half, j, far, s)
+        wait_rx(piece, rx)
 
     holder = half == (z // 2) % 2
     lane = core == z // 4
@@ -153,8 +167,8 @@
         wait_rx(col.at[m], col_rx.at[m], jnp.logical_not(lane))
 
     outs = [local(slab, slab_out, loc.at[0]), local(col, col_out, loc.at[1])]
-    for leg in (0, 1):
-        wait_rx(other.at[leg], other_rx.at[leg])
+    for i in range(8):
+        wait_rx(other.at[i], other_rx.at[i])
     outs.append(local(other, other_out, loc.at[2]))
     for copy in outs:
         copy.wait()
@@ -172,22 +186,21 @@
         move_kernel,
         out_shape=(jax.ShapeDtypeStruct((2, 2, 4, 128, 256), f32),
                    jax.ShapeDtypeStruct((4, 2, 128, 256), f32),
-                   jax.ShapeDtypeStruct((2, 256, 256), f32)),
+                   jax.ShapeDtypeStruct((8, 64, 256), f32)),
         in_specs=[any_spec],
         out_specs=(any_spec, any_spec, any_spec),
         scratch_shapes=[
             pltpu.VMEM((2, 2, 4, 128, 256), f32),
             pltpu.VMEM((4, 2, 128, 256), f32),
-            pltpu.VMEM((128, 256), f32),
-            pltpu.VMEM((2, 256, 256), f32),
-            pltpu.VMEM((2, 256, 256), f32),
-            pltpu.SemaphoreType.DMA((2, 2, 4)),
+            pltpu.VMEM((PARTS, 128 // PARTS, 256), f32),
+            pltpu.VMEM((8, 64, 256), f32),
+            pltpu.SemaphoreType.DMA((2, 2, 4, PARTS)),
             pltpu.SemaphoreType.DMA((4,)),
-            pltpu.SemaphoreType.DMA,
-            pltpu.SemaphoreType.DMA((2,)),
-            pltpu.SemaphoreType.DMA((2,)),
-            pltpu.SemaphoreType.DMA((48,)),
+            pltpu.SemaphoreType.DMA((PARTS,)),
+            pltpu.SemaphoreType.DMA((8,)),
+            pltpu.SemaphoreType.DMA((32 + 32 * PARTS,)),
             pltpu.SemaphoreType.DMA((4,)),
+            pltpu.SemaphoreType.DMA((PARTS,)),
         ],
         compiler_params=pltpu.CompilerParams(collective_id=0, has_side_effects=True),
     )(child_tile)
@@ -274,7 +287,7 @@
                          fac_high[768:], fac_low[768:])
             row_weights = [weights(maps, k, 2 * slab_index + t) for k in (0, 1)]
             own = [child[pl.ds(half * 512 + t * 256 + i * BLK, BLK), :] for i in (0, 1)]
-            sent = [other[t, i * BLK:(i + 1) * BLK, :] for i in (0, 1)]
+            sent = [other[4 * t + 2 * i:4 * t + 2 * i + 2].reshape(BLK, 256) for i in (0, 1)]
             ordered = [[jnp.where(half == k, a, b) for a, b in zip(own, sent)] for k in (0, 1)]
             blocks = expand(ordered, row_weights, col_weights)
             for p in range(3):

time: 162 us -> 137 us (0.85)
  the two profiles are of different devices: /device:TPU:224 before, /device:TPU:244 now
where the time goes in v3:
time: 137 us; the launch traced here: 136 us
  Pallas kernels  130 us (95%)
  local copies, waits for them, and re-layouts  6.54 us (5%)
    pallas_call x1, Pallas kernels, move(): pl.pallas_call(move_kernel, out_shape=(jax.ShapeDtypeStruct((2, 2, 4, 128...  117 us
    pallas_call x1, Pallas kernels, local(): pl.pallas_call(front_kernel, out_shape=jax.ShapeDtypeStruct((768, 384), j...  12.4 us
    unnamed x11, local copies, waits for them, and re-layouts  6.54 us

profile of v3, /device:TPU:244, one launch (start us, length us, event | category | flops | bytes accessed | tf_op | source)
XLA Modules:
  0.0 136.2 jit_solution(10834606356384226320)
XLA Ops:
  0.0 0.8 copy.5.pattern
  0.8 117.3 %shard_map.46 = (f32[2,2,4,128,256]{4,3,2,1,0:T(8,128)}, f32[4,2,128,256]{3,2,1,0:T(8,128)}, f32[8,64,256]{2,1,0:T(8,128)}) custom-call(f32[1024,256]{1,0:T(8,128)} %bitcast.2), custom_call_target="tpu_custom_call" | custom-call | tf_op jit(solution)/shard_map/pallas_call | solution.py:185
  118.1 0.0 copy-start
  118.1 1.2 copy-done
  119.3 0.0 copy-start.1
  119.3 1.6 %copy-done.1 = f32[2,2,4,128,256]{4,3,2,1,0:T(8,128)S(1)} copy-done((f32[2,2,4,128,256]{4,3,2,1,0:T(8,128)S(1)}, f32[2,2,4,128,256]{4,3,2,1,0:T(8,128)}, u32[]{:S(2)}) %copy-start.1) | copy-done | bytes 2097176
  120.9 0.0 copy-start.2
  120.9 1.2 copy-done.2
  122.1 0.0 copy-start.3
  122.1 1.0 copy-done.3
  123.1 0.0 copy-start.4
  123.1 0.7 copy-done.4
  123.8 12.4 %shard_map.47 = f32[768,384]{1,0:T(8,128)} custom-call(s32[2,64]{1,0:T(2,128)S(1)} %copy-done.4, s32[96,6]{1,0:T(8,128)S(1)} %copy.5.pattern, f32[768,768]{1,0:T(8,128)} %inverse.1, f32[1024,256]{1,0:T(8,128)S(1)} %bitcast.3, f32[8,64,256]{2,1,0:T(8,128)S(1)} %copy-done.3, f32[2,2,4,128,256]{4,3,2,1,0:T(8,128)S(1)} %copy-done.1, f32[4,2,128,256]{3,2,1,0:T(8,128)S(1)} %copy-done.2), custom_call_target="tpu_custom_call" | custom-call | tf_op jit(solution)/shard_map/pallas_call | solution.py:306
Async XLA Ops:
  118.1 1.2 copy-start
  119.3 1.6 %copy-start.1 = (f32[2,2,4,128,256]{4,3,2,1,0:T(8,128)S(1)}, f32[2,2,4,128,256]{4,3,2,1,0:T(8,128)}, u32[]{:S(2)}) copy-start(f32[2,2,4,128,256]{4,3,2,1,0:T(8,128)} %get-tuple-element.9.slab) | copy-start | bytes 6291460
  120.9 1.2 copy-start.2
  122.1 1.0 copy-start.3
  123.1 0.7 copy-start.4

commit v4 on v3

--- a/solution.py
+++ b/solution.py
@@ -140,6 +140,8 @@
         piece, rx = piece_of(half if own else 1 - half, j, far, s)
         wait_rx(piece, rx)
 
+    slab_done = local(slab, slab_out, cross_loc.at[0])
+
     holder = half == (z // 2) % 2
     lane = core == z // 4
     owner = holder & lane & (y == x)
@@ -166,7 +168,7 @@
     for m in range(4):
         wait_rx(col.at[m], col_rx.at[m], jnp.logical_not(lane))
 
-    outs = [local(slab, slab_out, loc.at[0]), local(col, col_out, loc.at[1])]
+    outs = [slab_done, local(col, col_out, loc.at[1])]
     for i in range(8):
         wait_rx(other.at[i], other_rx.at[i])
     outs.append(local(other, other_out, loc.at[2]))
@@ -234,17 +236,26 @@
     return total
 
 
-def front_kernel(maps, pattern, inverse, child, other, slab, col, out,
-                 inv_high, inv_low, tile_high, tile_low, fac_high, fac_low):
+def front_kernel(maps, pattern, inverse_in, child_in, other_in, slab_in, col_in, out,
+                 inverse, child, other, slab, col, arrived, inv_high, inv_low, tile_high, tile_low, fac_high, fac_low):
     half = lax.axis_index("half")
     row = lax.axis_index("row")
     colix = lax.axis_index("col")
     slab_index = 2 * row + half
+    copies = [pltpu.make_async_copy(src, dst, arrived.at[i]) for i, (src, dst) in enumerate((
+        (inverse_in, inverse), (slab_in, slab), (col_in, col),
+        (child_in.at[pl.ds(half * 512, 512)], child), (other_in, other)))]
+    for copy in copies:
+        copy.start()
+    copies[0].wait()
     for b in range(6):
         rows = slice(b * BLK, (b + 1) * BLK)
         inv_high[rows], inv_low[rows] = split(inverse[rows])
+    copies[1].wait()
     panel_cols = [[weights(maps, k, j) for k in (0, 1)] for j in (0, 1)]
     for t in range(3):
+        if t == 2:
+            copies[2].wait()
         triple = 2 * slab_index + t if t < 2 else colix
         row_weights = [weights(maps, k, triple) for k in (0, 1)]
         for j in range(2):
@@ -278,6 +289,9 @@
                         def _(rows=rows, b=b, block=block):
                             out[rows, (b % 3) * BLK:(b % 3 + 1) * BLK] = block
 
+    copies[3].wait()
+    copies[4].wait()
+
     @pl.when(colix >= 2)
     def _():
         col_weights = [weights(maps, k, colix) for k in (0, 1)]
@@ -286,7 +300,7 @@
             schur = dot3(fac_high[t * 384:(t + 1) * 384], fac_low[t * 384:(t + 1) * 384],
                          fac_high[768:], fac_low[768:])
             row_weights = [weights(maps, k, 2 * slab_index + t) for k in (0, 1)]
-            own = [child[pl.ds(half * 512 + t * 256 + i * BLK, BLK), :] for i in (0, 1)]
+            own = [child[t * 256 + i * BLK:t * 256 + (i + 1) * BLK, :] for i in (0, 1)]
             sent = [other[4 * t + 2 * i:4 * t + 2 * i + 2].reshape(BLK, 256) for i in (0, 1)]
             ordered = [[jnp.where(half == k, a, b) for a, b in zip(own, sent)] for k in (0, 1)]
             blocks = expand(ordered, row_weights, col_weights)
@@ -302,13 +316,20 @@
     slab, col, other = move(child_tile)
     smem = pl.BlockSpec(memory_space=pltpu.SMEM)
     vmem = pl.BlockSpec(memory_space=pltpu.VMEM)
-    bf16 = jnp.bfloat16
+    bf16, f32 = jnp.bfloat16, jnp.float32
+    hbm = pl.BlockSpec(memory_space=pl.ANY)
     result = pl.pallas_call(
         front_kernel,
         out_shape=jax.ShapeDtypeStruct((768, 384), jnp.float32),
-        in_specs=[smem, smem] + [vmem] * 5,
+        in_specs=[smem, smem] + [hbm] * 5,
         out_specs=vmem,
         scratch_shapes=[
+            pltpu.VMEM((768, 768), f32),
+            pltpu.VMEM((512, 256), f32),
+            pltpu.VMEM((8, 64, 256), f32),
+            pltpu.VMEM((2, 2, 4, 128, 256), f32),
+            pltpu.VMEM((4, 2, 128, 256), f32),
+            pltpu.SemaphoreType.DMA((5,)),
             pltpu.VMEM((768, 768), bf16),
             pltpu.VMEM((768, 768), bf16),
             pltpu.VMEM((3, 384, 768), bf16),
@@ -316,7 +337,7 @@
             pltpu.VMEM((1152, 768), bf16),
             pltpu.VMEM((1152, 768), bf16),
         ],
-        compiler_params=pltpu.CompilerParams(vmem_limit_bytes=48 * 2**20),
+        compiler_params=pltpu.CompilerParams(vmem_limit_bytes=60 * 2**20),
     )(child_maps, panel_pattern, pivot_inverse, child_tile, other, slab, col)
     return result.reshape(1, 1, 768, 384)
 

time: 137 us -> 133 us (0.971)
  local copies, waits for them, and re-layouts: 6.54 us -> 1.4 us
    unnamed x11 -> x1, local copies, waits for them, and re-layouts: 6.54 us -> 1.4 us
    pallas_call x1, Pallas kernels: 12.4 us -> 14.2 us  [local(): pl.pallas_call(front_kernel, out_shape=jax.ShapeDtypeStruct((768, 384), j...]
where the time goes in v4:
time: 133 us; the launch traced here: 132 us
  Pallas kernels  131 us (98%)
  local copies, waits for them, and re-layouts  1.4 us (1%)
    pallas_call x1, Pallas kernels, move(): pl.pallas_call(move_kernel, out_shape=(jax.ShapeDtypeStruct((2, 2, 4, 128...  117 us
    pallas_call x1, Pallas kernels, local(): pl.pallas_call(front_kernel, out_shape=jax.ShapeDtypeStruct((768, 384), j...  14.2 us

profile of v4, /device:TPU:244, one launch (start us, length us, event | category | flops | bytes accessed | tf_op | source)
XLA Modules:
  0.0 132.2 jit_solution(8292577178184325712)
XLA Ops:
  0.0 1.4 %copy.5.pattern = s32[96,6]{1,0:T(8,128)} copy(s32[96,6]{0,1:T(8,128)} %param.6) | data formatting | bytes 4608 | tf_op args[2]
  1.4 116.6 %shard_map.46 = (f32[2,2,4,128,256]{4,3,2,1,0:T(8,128)}, f32[4,2,128,256]{3,2,1,0:T(8,128)}, f32[8,64,256]{2,1,0:T(8,128)}) custom-call(f32[1024,256]{1,0:T(8,128)} %bitcast.2), custom_call_target="tpu_custom_call" | custom-call | tf_op jit(solution)/shard_map/pallas_call | solution.py:187
  118.0 14.2 %shard_map.47 = f32[768,384]{1,0:T(8,128)} custom-call(s32[2,64]{1,0:T(2,128)} %maps.1, s32[96,6]{1,0:T(8,128)} %copy.5.pattern, f32[768,768]{1,0:T(8,128)} %inverse_in.1, f32[1024,256]{1,0:T(8,128)} %bitcast.3, f32[8,64,256]{2,1,0:T(8,128)} %get-tuple-element.8.other_in, f32[2,2,4,128,256]{4,3,2,1,0:T(8,128)} %get-tuple-element.9.slab_in, ...), custom_call_target="tpu_custom_call" | custom-call | tf_op jit(solution)/shard_map/pallas_call | solution.py:321
